TPU v7x, 256 devices: a whole 4x4x8 slice. The times are simulated.
256 devices in a mesh: section: 4 (over x), dp: 16 (over y_hi, z), tensor: 4 (over y_lo, core).
Axes of the slice: x: 4, y: 4 (y_hi: 2, y_lo: 2; y = y_hi * 2 + y_lo), z: 8, core: 2. Of those that a mesh axis runs over, the one named last changes fastest.
Arguments:
- enc_input: bfloat16 [2, 16, 128, 4096], P(None, 'dp', None, 'tensor'), may hold values from -10.8 to 10.8
- dec_input: bfloat16 [2, 16, 128, 4096], P(None, 'dp', None, 'tensor'), may hold values from -6 to 6
- lengths: int32 [2, 2, 16], P(None, None, 'dp'), may hold values from 16 to 128, as said below
- offset_bucket: int32 [2, 255], replicated, may hold values from 0 to 31
- bias_tables: float32 [2, 32, 32], P(None, None, 'tensor'), may hold values from -4.5 to 303
- norm_gain: float32 [4, 4096], P('section'), may hold values from 0.5 to 1.5
- final_gain: float32 [4096], P('tensor'), may hold values from 0.5 to 1.5
- w_query: bfloat16 [4, 4096, 2048], P('section', 'dp', 'tensor'), may hold values from -0.0234375 to 0.0234375
- w_key: bfloat16 [4, 4096, 2048], P('section', 'dp', 'tensor'), may hold values from -0.09375 to 0.09375
- w_value: bfloat16 [4, 4096, 2048], P('section', 'dp', 'tensor'), may hold values from -0.09375 to 0.09375
- w_out: bfloat16 [4, 2048, 4096], P('section', 'tensor', 'dp'), may hold values from -0.125 to 0.125
Outputs:
- section_out: bfloat16 [4, 2, 16, 128, 4096], P('section', None, 'dp', None, 'tensor')
Inputs may be any that keep to these rules, and one draw needn't show every extreme that they name: In every micro-batch, sequence 0 has both lengths equal to 128.
All inputs are finite; a program needn't handle non-finite values.
Results may differ from a plain program's by a relative error of at most 0.02.
Values may be sent and summed in bfloat16 or wider, within the bound.
No kernel may reach another device: no remote copies, remote signals or barrier semaphores. Data moves between devices by JAX's collectives and lax.ppermute only.
A program may use at most 128 MiB of HBM per device.

v0:
```python
import jax
import jax.numpy as jnp
from jax import lax
from jax.sharding import PartitionSpec as P

D = 4096
HEAD_DIM = 64


def shifted(value, axis, steps):
    count = lax.axis_size(axis)
    initial, last = (max(0, -steps), min(count, count - steps))
    return lax.ppermute(value, axis, [(source, source + steps) for source in range(initial, last)])


def positional_bias(offset_bucket, bias_tables, section_id, length):
    bucket_row = jnp.where(section_id == 0, offset_bucket[0], offset_bucket[1])
    tables = jnp.where(section_id == 0, bias_tables[0], bias_tables[1])
    tables = tables * jnp.where(section_id == 2, 0.0, 1.0).astype(jnp.float32)
    query_pos = lax.broadcasted_iota(jnp.int32, (length, length), 0)
    key_pos = lax.broadcasted_iota(jnp.int32, (length, length), 1)
    bucket = jnp.take(bucket_row, key_pos - query_pos + (length - 1))
    bucket_ids = lax.broadcasted_iota(jnp.int32, (1, 1, tables.shape[0]), 2)
    onehot = (bucket[:, :, None] == bucket_ids).astype(jnp.float32)
    return jnp.einsum("qkb,bh->hqk", onehot, tables, precision=lax.Precision.HIGHEST)


def attend_local(
    layer_normed,
    encoder_memory,
    complete_query,
    complete_key,
    complete_value,
    complete_output,
    score_bias,
    allowed,
):
    seq_count, length, width = layer_normed.shape
    queries = jnp.einsum(
        "vyt,te->vye", layer_normed, complete_query, preferred_element_type=jnp.float32
    ).astype(jnp.bfloat16)
    keys_proj = jnp.einsum(
        "vyt,te->vye", encoder_memory, complete_key, preferred_element_type=jnp.float32
    ).astype(jnp.bfloat16)
    values = jnp.einsum(
        "vyt,te->vye", encoder_memory, complete_value, preferred_element_type=jnp.float32
    ).astype(jnp.bfloat16)
    head_count = queries.shape[2] // HEAD_DIM
    query_heads = queries.reshape(seq_count, length, head_count, HEAD_DIM)
    key_heads = keys_proj.reshape(seq_count, length, head_count, HEAD_DIM)
    value_heads = values.reshape(seq_count, length, head_count, HEAD_DIM)
    scores = jnp.einsum(
        "sqhc,skhc->shqk", query_heads, key_heads, preferred_element_type=jnp.float32
    )
    scores = scores + score_bias[None]
    scores = jnp.where(allowed[:, None], scores, -1e30)
    highest = jnp.max(scores, axis=-1, keepdims=True)
    expsum = jnp.exp(scores - highest)
    weights_bf = (expsum / jnp.sum(expsum, axis=-1, keepdims=True)).astype(jnp.bfloat16)
    attended_context = jnp.einsum(
        "shqk,skhc->sqhc", weights_bf, value_heads, preferred_element_type=jnp.float32
    ).astype(jnp.bfloat16)
    attended_context = attended_context.reshape(seq_count, length, head_count * HEAD_DIM)
    return jnp.einsum(
        "bqf,fw->bqw", attended_context, complete_output, preferred_element_type=jnp.float32
    )


def body(
    enc_input,
    dec_input,
    lengths,
    offset_bucket,
    bias_tables,
    norm_gain,
    final_gain,
    w_query,
    w_key,
    w_value,
    w_out,
):
    section_id = lax.axis_index("section")
    micro_count, seq_count, length, quarter = enc_input.shape
    complete_query, complete_key, complete_value, complete_output = (
        lax.all_gather(w_query[0], "dp", axis=0, tiled=True),
        lax.all_gather(w_key[0], "dp", axis=0, tiled=True),
        lax.all_gather(w_value[0], "dp", axis=0, tiled=True),
        lax.all_gather(w_out[0], "dp", axis=1, tiled=True),
    )
    score_bias = positional_bias(offset_bucket, bias_tables, section_id, length)
    query_pos = lax.broadcasted_iota(jnp.int32, (length, length), 0)
    key_pos = lax.broadcasted_iota(jnp.int32, (length, length), 1)
    causal = jnp.logical_or(section_id == 1, section_id == 3)
    encoder_keys = jnp.logical_or(section_id == 0, section_id == 2)
    order_ok = jnp.logical_or(jnp.logical_not(causal), key_pos <= query_pos)
    gain_full = norm_gain[0]
    tick_count = micro_count + lax.axis_size("section") - 1
    zero_block = jnp.zeros((seq_count, length, quarter), jnp.bfloat16)
    carry_h = zero_block
    carry_e = zero_block
    record = jnp.zeros((micro_count, seq_count, length, quarter), jnp.bfloat16)
    for moment in range(tick_count):
        offset = moment - section_id
        active = jnp.logical_and(offset >= 0, offset < micro_count)
        micro_id = jnp.clip(offset, 0, micro_count - 1)
        enc_now = lax.dynamic_index_in_dim(enc_input, micro_id, 0, keepdims=False)
        dec_now = lax.dynamic_index_in_dim(dec_input, micro_id, 0, keepdims=False)
        input_rows = jnp.where(
            section_id == 0, enc_now, jnp.where(section_id == 1, dec_now, carry_h)
        )
        length_pair = lax.dynamic_index_in_dim(lengths, micro_id, 0, keepdims=False)
        key_len = jnp.where(encoder_keys, length_pair[0], length_pair[1])
        allowed = jnp.logical_and(key_pos[None] < key_len[:, None, None], order_ok[None])
        memory_part = carry_e
        gathered, memory_whole = (
            lax.all_gather(input_rows, "tensor", axis=2, tiled=True),
            lax.all_gather(memory_part, "tensor", axis=2, tiled=True),
        )
        single = gathered.astype(jnp.float32)
        mean_sq = jnp.mean(single * single, axis=-1, keepdims=True)
        layer_normed = (single * lax.rsqrt(mean_sq + 1e-06) * gain_full).astype(jnp.bfloat16)
        encoder_memory = jnp.where(section_id == 2, memory_whole, layer_normed)
        partial_value = attend_local(
            layer_normed,
            encoder_memory,
            complete_query,
            complete_key,
            complete_value,
            complete_output,
            score_bias,
            allowed,
        )
        shared = lax.psum_scatter(
            partial_value.astype(jnp.bfloat16), "tensor", scatter_dimension=2, tiled=True
        ).astype(jnp.float32)
        hidden_wide = input_rows.astype(jnp.float32) + shared
        hidden = hidden_wide.astype(jnp.bfloat16)
        hidden_back = hidden.astype(jnp.float32)
        enc_square = lax.psum(jnp.sum(hidden_back * hidden_back, axis=-1), "tensor")
        enc_out = (hidden_back * lax.rsqrt(enc_square / D + 1e-06)[:, :, None] * final_gain).astype(
            jnp.bfloat16
        )
        result = jnp.where(section_id == 0, enc_out, hidden)
        current = lax.dynamic_index_in_dim(record, micro_id, 0, keepdims=False)
        record = lax.dynamic_update_index_in_dim(
            record, jnp.where(active, result, current), micro_id, 0
        )
        if moment + 1 < tick_count:
            enc_pass = jnp.where(section_id == 0, enc_out, carry_e)
            carry_h, carry_e = shifted((result, enc_pass), "section", 1)
    return record[None]


def solution(mesh):
    in_specs = (
        P(None, "dp", None, "tensor"),
        P(None, "dp", None, "tensor"),
        P(None, None, "dp"),
        P(),
        P(None, None, "tensor"),
        P("section", None),
        P("tensor"),
        P("section", "dp", "tensor"),
        P("section", "dp", "tensor"),
        P("section", "dp", "tensor"),
        P("section", "tensor", "dp"),
    )
    out_specs = P("section", None, "dp", None, "tensor")
    return jax.shard_map(body, mesh=mesh, in_specs=in_specs, out_specs=out_specs, check_vma=False)
```

profile of v0, /device:TPU:1, one launch (start us, length us, event | category | flops | bytes accessed | tf_op | source)
XLA Modules:
  0.0 913.5 jit_solution(5208827000141781013)
XLA Ops:
  6.5 1.8 select_select_fusion
  11.1 101.4 %gather_fusion = s32[16384]{0:T(1024)S(1)} fusion(s32[255]{0:T(256)S(1)} %bitcast.319, s32[16384]{0:T(1024)S(1)} %fusion.172), kind=kCustom, calls=%fused_computation | custom fusion | bytes 196608 | tf_op jit(solution)/shard_map/jit(_take)/gather | solution.py:22
  115.6 1.5 fusion.57
  117.2 18.8 %all-gather.37.cloned.1.call-done = bf16[1,4096,512]{2,1,0:T(8,128)(2,1)} async-done(((bf16[1,256,512]{2,1,0:T(8,128)(2,1)}), bf16[1,4096,512]{2,1,0:T(8,128)(2,1)}) %all-gather.37.cloned.1.call-update) | async-done | bytes 4194320 | tf_op jit(solution)/shard_map/all_gather | solution.py:87
  136.0 3.4 fusion.76
  139.5 95.5 %all-gather.39.cloned.1.call-done = bf16[1,4096,512]{2,1,0:T(8,128)(2,1)} async-done(((bf16[1,256,512]{2,1,0:T(8,128)(2,1)}), bf16[1,4096,512]{2,1,0:T(8,128)(2,1)}) %all-gather.39.cloned.1.call-update) | async-done | bytes 4194320 | tf_op jit(solution)/shard_map/all_gather | solution.py:85
  235.0 3.0 fusion.91
  238.1 95.7 %all-gather.41.cloned.1.call-done = bf16[1,4096,512]{2,1,0:T(8,128)(2,1)} async-done(((bf16[1,256,512]{2,1,0:T(8,128)(2,1)}), bf16[1,4096,512]{2,1,0:T(8,128)(2,1)}) %all-gather.41.cloned.1.call-update) | async-done | bytes 4194320 | tf_op jit(solution)/shard_map/all_gather | solution.py:86
  333.8 3.0 fusion.106
  337.6 100.2 %all-gather.43.cloned.1.call-done = bf16[1,512,4096]{2,1,0:T(8,128)(2,1)} async-done(((bf16[1,512,256]{2,1,0:T(8,128)(2,1)}), bf16[1,512,4096]{2,1,0:T(8,128)(2,1)}) %all-gather.43.cloned.1.call-update) | async-done | bytes 4194320 | tf_op jit(solution)/shard_map/all_gather | solution.py:88
  437.8 4.0 fusion.5
  441.9 23.7 %reduce-scatter.6.cloned.1.call-done = bf16[1,128,1024]{2,1,0:T(8,128)(2,1)} async-done(((bf16[1,128,4096]{2,1,0:T(8,128)(2,1)}), bf16[1,128,1024]{2,1,0:T(8,128)(2,1)}) %reduce-scatter.6.cloned.1.call-update) | async-done | bytes 262160 | tf_op jit(solution)/shard_map/reduce_scatter | solution.py:133
  466.7 5.1 psum.35
  473.0 3.1 collective-permute-start
  476.2 4.3 collective-permute-done
  481.5 4.1 collective-permute-start.1
  485.6 3.3 collective-permute-done.1
  492.2 16.3 %all-gather.21.cloned.1.call-done = bf16[1,128,4096]{2,1,0:T(8,128)(2,1)} async-done(((bf16[1,128,1024]{2,1,0:T(8,128)(2,1)}), bf16[1,128,4096]{2,1,0:T(8,128)(2,1)}) %all-gather.21.cloned.1.call-update) | async-done | bytes 1048592 | tf_op jit(solution)/shard_map/all_gather | solution.py:116
  508.5 1.5 fusion.45
  510.1 24.4 %all-gather.19.cloned.1.call-done = bf16[1,128,4096]{2,1,0:T(8,128)(2,1)} async-done(((bf16[1,128,1024]{2,1,0:T(8,128)(2,1)}), bf16[1,128,4096]{2,1,0:T(8,128)(2,1)}) %all-gather.19.cloned.1.call-update) | async-done | bytes 1048592 | tf_op jit(solution)/shard_map/all_gather | solution.py:117
  534.5 3.3 fusion.79
  537.9 3.0 fusion.94
  541.0 3.0 fusion.109
  545.5 4.0 fusion.6
  549.6 24.5 %reduce-scatter.8.cloned.1.call-done = bf16[1,128,1024]{2,1,0:T(8,128)(2,1)} async-done(((bf16[1,128,4096]{2,1,0:T(8,128)(2,1)}), bf16[1,128,1024]{2,1,0:T(8,128)(2,1)}) %reduce-scatter.8.cloned.1.call-update) | async-done | bytes 262160 | tf_op jit(solution)/shard_map/reduce_scatter | solution.py:133
  575.3 5.1 psum.36
  581.6 3.1 collective-permute-start.2
  584.7 4.3 collective-permute-done.2
  590.0 4.1 collective-permute-start.3
  594.1 3.3 collective-permute-done.3
  600.3 16.8 %all-gather.25.cloned.1.call-done = bf16[1,128,4096]{2,1,0:T(8,128)(2,1)} async-done(((bf16[1,128,1024]{2,1,0:T(8,128)(2,1)}), bf16[1,128,4096]{2,1,0:T(8,128)(2,1)}) %all-gather.25.cloned.1.call-update) | async-done | bytes 1048592 | tf_op jit(solution)/shard_map/all_gather | solution.py:116
  618.6 24.4 %all-gather.23.cloned.1.call-done = bf16[1,128,4096]{2,1,0:T(8,128)(2,1)} async-done(((bf16[1,128,1024]{2,1,0:T(8,128)(2,1)}), bf16[1,128,4096]{2,1,0:T(8,128)(2,1)}) %all-gather.23.cloned.1.call-update) | async-done | bytes 1048592 | tf_op jit(solution)/shard_map/all_gather | solution.py:117
  643.0 3.3 fusion.82
  646.4 3.0 fusion.97
  649.5 3.0 fusion.112
  654.0 4.0 fusion.7
  658.1 24.5 %reduce-scatter.10.cloned.1.call-done = bf16[1,128,1024]{2,1,0:T(8,128)(2,1)} async-done(((bf16[1,128,4096]{2,1,0:T(8,128)(2,1)}), bf16[1,128,1024]{2,1,0:T(8,128)(2,1)}) %reduce-scatter.10.cloned.1.call-update) | async-done | bytes 262160 | tf_op jit(solution)/shard_map/reduce_scatter | solution.py:133
  683.8 5.1 psum.37
  690.1 3.1 collective-permute-start.4
  693.2 4.3 collective-permute-done.4
  698.6 4.1 collective-permute-start.5
  702.7 3.3 collective-permute-done.5
  709.3 16.3 %all-gather.29.cloned.1.call-done = bf16[1,128,4096]{2,1,0:T(8,128)(2,1)} async-done(((bf16[1,128,1024]{2,1,0:T(8,128)(2,1)}), bf16[1,128,4096]{2,1,0:T(8,128)(2,1)}) %all-gather.29.cloned.1.call-update) | async-done | bytes 1048592 | tf_op jit(solution)/shard_map/all_gather | solution.py:116
  725.6 1.5 fusion.51
  727.1 24.3 %all-gather.27.cloned.1.call-done = bf16[1,128,4096]{2,1,0:T(8,128)(2,1)} async-done(((bf16[1,128,1024]{2,1,0:T(8,128)(2,1)}), bf16[1,128,4096]{2,1,0:T(8,128)(2,1)}) %all-gather.27.cloned.1.call-update) | async-done | bytes 1048592 | tf_op jit(solution)/shard_map/all_gather | solution.py:117
  751.4 3.3 fusion.85
  754.8 3.0 fusion.100
  757.9 3.0 fusion.115
  762.4 4.0 fusion.8
  766.5 24.5 %reduce-scatter.12.cloned.1.call-done = bf16[1,128,1024]{2,1,0:T(8,128)(2,1)} async-done(((bf16[1,128,4096]{2,1,0:T(8,128)(2,1)}), bf16[1,128,1024]{2,1,0:T(8,128)(2,1)}) %reduce-scatter.12.cloned.1.call-update) | async-done | bytes 262160 | tf_op jit(solution)/shard_map/reduce_scatter | solution.py:133
  792.2 5.1 psum.38
  798.5 3.1 collective-permute-start.6
  801.6 4.3 collective-permute-done.6
  806.9 4.1 collective-permute-start.7
  811.0 3.3 collective-permute-done.7
  816.7 17.3 %all-gather.33.cloned.1.call-done = bf16[1,128,4096]{2,1,0:T(8,128)(2,1)} async-done(((bf16[1,128,1024]{2,1,0:T(8,128)(2,1)}), bf16[1,128,4096]{2,1,0:T(8,128)(2,1)}) %all-gather.33.cloned.1.call-update) | async-done | bytes 1048592 | tf_op jit(solution)/shard_map/all_gather | solution.py:116
  835.5 24.3 %all-gather.31.cloned.1.call-done = bf16[1,128,4096]{2,1,0:T(8,128)(2,1)} async-done(((bf16[1,128,1024]{2,1,0:T(8,128)(2,1)}), bf16[1,128,4096]{2,1,0:T(8,128)(2,1)}) %all-gather.31.cloned.1.call-update) | async-done | bytes 1048592 | tf_op jit(solution)/shard_map/all_gather | solution.py:117
  859.7 3.3 fusion.88
  863.2 3.0 fusion.103
  866.2 3.0 fusion.118
  870.0 3.9 fusion.9
  874.8 23.8 %reduce-scatter.14.cloned.1.call-done = bf16[1,128,1024]{2,1,0:T(8,128)(2,1)} async-done(((bf16[1,128,4096]{2,1,0:T(8,128)(2,1)}), bf16[1,128,1024]{2,1,0:T(8,128)(2,1)}) %reduce-scatter.14.cloned.1.call-update) | async-done | bytes 262160 | tf_op jit(solution)/shard_map/reduce_scatter | solution.py:133
  899.7 5.1 psum.39
  904.8 1.8 fusion.166
  (177 shorter events, 36.9 us)
Async XLA Ops:
  6.5 4.5 copy-start.26
  6.5 109.1 %all-gather.35.cloned.1.call-start = ((), (), s32[]{:S(2)}) async-start(), calls=%async_computation.18 | async-start | bytes 1310720 | tf_op jit(solution)/shard_map/all_gather | solution.py:116
  8.3 127.7 %all-gather.37.cloned.1.call-start = ((), (), s32[]{:S(2)}) async-start(), calls=%async_computation.19 | async-start | bytes 4456448 | tf_op jit(solution)/shard_map/all_gather | solution.py:87
  9.1 225.9 %all-gather.39.cloned.1.call-start = ((), (), s32[]{:S(2)}) async-start(), calls=%async_computation.20 | async-start | bytes 4456448 | tf_op jit(solution)/shard_map/all_gather | solution.py:85
  9.8 324.0 %all-gather.41.cloned.1.call-start = ((), (), s32[]{:S(2)}) async-start(), calls=%async_computation.21 | async-start | bytes 4456448 | tf_op jit(solution)/shard_map/all_gather | solution.py:86
  10.4 427.4 %all-gather.43.cloned.1.call-start = ((), (), s32[]{:S(2)}) async-start(), calls=%async_computation.22 | async-start | bytes 4456448 | tf_op jit(solution)/shard_map/all_gather | solution.py:88
  11.0 454.5 %reduce-scatter.6.cloned.1.call-start = ((), (), s32[]{:S(2)}) async-start(), calls=%async_computation.5 | async-start | bytes 1310720 | tf_op jit(solution)/shard_map/reduce_scatter | solution.py:133
  11.1 101.5 %copy-start.25 = (f32[2,32,8]{1,2,0:T(8,128)S(1)}, f32[2,32,8]{1,2,0:T(8,128)}, u32[]{:S(2)}) copy-start(f32[2,32,8]{1,2,0:T(8,128)} %param.15) | copy-start | bytes 6148
  11.1 102.5 %copy-start.24 = (s32[2,2,1]{1,2,0:T(1,128)S(1)}, s32[2,2,1]{1,2,0:T(1,128)}, u32[]{:S(2)}) copy-start(s32[2,2,1]{1,2,0:T(1,128)} %param.13) | copy-start | bytes 52
  112.5 23.5 %copy-start.27 = (f32[1,4096]{1,0:T(1,128)S(1)}, f32[1,4096]{1,0:T(1,128)}, u32[]{:S(2)}) copy-start(f32[1,4096]{1,0:T(1,128)} %param.16) | copy-start | bytes 49156
  136.0 99.0 %copy-start.17 = (bf16[1,1,128,4096]{3,2,1,0:T(8,128)(2,1)S(1)}, bf16[1,1,128,4096]{3,2,1,0:T(8,128)(2,1)}, u32[]{:S(2)}) copy-start(bf16[1,1,128,4096]{3,2,1,0:T(8,128)(2,1)} %all-gather.35.cloned.1.call-done) | copy-start | bytes 3145732
  437.8 27.7 %copy-start.3 = (bf16[1,1,128,1024]{3,2,1,0:T(8,128)(2,1)S(1)}, bf16[1,1,128,1024]{3,2,1,0:T(8,128)(2,1)}, u32[]{:S(2)}) copy-start(bf16[1,1,128,1024]{3,2,1,0:T(8,128)(2,1)} %select_select_fusion) | copy-start | bytes 786436
  441.8 30.1 %copy-start.22 = (f32[1024]{0:T(1024)S(1)}, f32[1024]{0:T(1024)}, u32[]{:S(2)}) copy-start(f32[1024]{0:T(1024)} %param.17) | copy-start | bytes 12292
  441.8 38.7 %copy-start.5 = (bf16[2,1,128,1024]{3,2,1,0:T(8,128)(2,1)S(1)}, bf16[2,1,128,1024]{3,2,1,0:T(8,128)(2,1)}, u32[]{:S(2)}) copy-start(bf16[2,1,128,1024]{3,2,1,0:T(8,128)(2,1)} %param.12) | copy-start | bytes 1572868
  441.8 38.7 %copy-start.6 = (bf16[2,1,128,1024]{3,2,1,0:T(8,128)(2,1)S(1)}, bf16[2,1,128,1024]{3,2,1,0:T(8,128)(2,1)}, u32[]{:S(2)}) copy-start(bf16[2,1,128,1024]{3,2,1,0:T(8,128)(2,1)} %param.11) | copy-start | bytes 1572868
  441.8 66.7 %all-gather.21.cloned.1.call-start = ((), (), s32[]{:S(2)}) async-start(), calls=%async_computation.7 | async-start | bytes 1310720 | tf_op jit(solution)/shard_map/all_gather | solution.py:116
  465.5 15.8 %copy-start.10 = (bf16[1,128,1024]{2,1,0:T(8,128)(2,1)S(1)}, bf16[1,128,1024]{2,1,0:T(8,128)(2,1)}, u32[]{:S(2)}) copy-start(bf16[1,128,1024]{2,1,0:T(8,128)(2,1)} %reduce-scatter.6.cloned.1.call-done) | copy-start | bytes 786436
  473.0 7.5 collective-permute-start
  481.3 53.2 %all-gather.19.cloned.1.call-start = ((), (), s32[]{:S(2)}) async-start(), calls=%async_computation.6 | async-start | bytes 1310720 | tf_op jit(solution)/shard_map/all_gather | solution.py:117
  481.5 7.4 collective-permute-start.1
  488.9 0.7 copy-start.13
  489.6 84.5 %reduce-scatter.8.cloned.1.call-start = ((), (), s32[]{:S(2)}) async-start(), calls=%async_computation.8 | async-start | bytes 1310720 | tf_op jit(solution)/shard_map/reduce_scatter | solution.py:133
  510.1 27.8 %copy-start.20 = (bf16[1,128,4096]{2,1,0:T(8,128)(2,1)S(1)}, bf16[1,128,4096]{2,1,0:T(8,128)(2,1)}, u32[]{:S(2)}) copy-start(bf16[1,128,4096]{2,1,0:T(8,128)(2,1)} %all-gather.21.cloned.1.call-done) | copy-start | bytes 3145732
  545.5 28.6 %copy-start.1 = (bf16[1,128,1024]{2,1,0:T(8,128)(2,1)S(1)}, bf16[1,128,1024]{2,1,0:T(8,128)(2,1)}, u32[]{:S(2)}) copy-start(bf16[1,128,1024]{2,1,0:T(8,128)(2,1)} %fusion.170) | copy-start | bytes 786436
  549.5 40.3 %copy-start.14 = (bf16[1,128,1024]{2,1,0:T(8,128)(2,1)S(1)}, bf16[1,128,1024]{2,1,0:T(8,128)(2,1)}, u32[]{:S(2)}) copy-start(bf16[1,128,1024]{2,1,0:T(8,128)(2,1)} %copy-done.13) | copy-start | bytes 786436
  549.5 67.5 %all-gather.25.cloned.1.call-start = ((), (), s32[]{:S(2)}) async-start(), calls=%async_computation.10 | async-start | bytes 1310720 | tf_op jit(solution)/shard_map/all_gather | solution.py:116
  574.1 15.7 %copy-start.8 = (bf16[1,128,1024]{2,1,0:T(8,128)(2,1)S(1)}, bf16[1,128,1024]{2,1,0:T(8,128)(2,1)}, u32[]{:S(2)}) copy-start(bf16[1,128,1024]{2,1,0:T(8,128)(2,1)} %reduce-scatter.8.cloned.1.call-done) | copy-start | bytes 786436
  581.6 61.4 %copy-start.28 = (f32[1,4096]{1,0:T(1,128)S(1)}, f32[1,4096]{1,0:T(1,128)}, u32[]{:S(2)}) copy-start(f32[1,4096]{1,0:T(1,128)} %param.16) | copy-start | bytes 49156
  581.6 7.4 collective-permute-start.2
  589.8 53.2 %all-gather.23.cloned.1.call-start = ((), (), s32[]{:S(2)}) async-start(), calls=%async_computation.9 | async-start | bytes 1310720 | tf_op jit(solution)/shard_map/all_gather | solution.py:117
  590.0 7.4 collective-permute-start.3
  597.4 0.7 copy-start.15
  598.1 84.5 %reduce-scatter.10.cloned.1.call-start = ((), (), s32[]{:S(2)}) async-start(), calls=%async_computation.11 | async-start | bytes 1310720 | tf_op jit(solution)/shard_map/reduce_scatter | solution.py:133
  618.6 27.8 %copy-start.21 = (bf16[1,128,4096]{2,1,0:T(8,128)(2,1)S(1)}, bf16[1,128,4096]{2,1,0:T(8,128)(2,1)}, u32[]{:S(2)}) copy-start(bf16[1,128,4096]{2,1,0:T(8,128)(2,1)} %all-gather.25.cloned.1.call-done) | copy-start | bytes 3145732
  654.0 28.6 %copy-start.2 = (bf16[1,128,1024]{2,1,0:T(8,128)(2,1)S(1)}, bf16[1,128,1024]{2,1,0:T(8,128)(2,1)}, u32[]{:S(2)}) copy-start(bf16[1,128,1024]{2,1,0:T(8,128)(2,1)} %fusion.169) | copy-start | bytes 786436
  658.0 40.4 %copy-start.16 = (bf16[1,128,1024]{2,1,0:T(8,128)(2,1)S(1)}, bf16[1,128,1024]{2,1,0:T(8,128)(2,1)}, u32[]{:S(2)}) copy-start(bf16[1,128,1024]{2,1,0:T(8,128)(2,1)} %copy-done.15) | copy-start | bytes 786436
  658.0 67.5 %all-gather.29.cloned.1.call-start = ((), (), s32[]{:S(2)}) async-start(), calls=%async_computation.13 | async-start | bytes 1310720 | tf_op jit(solution)/shard_map/all_gather | solution.py:116
  682.6 15.8 %copy-start.9 = (bf16[1,128,1024]{2,1,0:T(8,128)(2,1)S(1)}, bf16[1,128,1024]{2,1,0:T(8,128)(2,1)}, u32[]{:S(2)}) copy-start(bf16[1,128,1024]{2,1,0:T(8,128)(2,1)} %reduce-scatter.10.cloned.1.call-done) | copy-start | bytes 786436
  690.1 61.3 %copy-start.29 = (f32[1,4096]{1,0:T(1,128)S(1)}, f32[1,4096]{1,0:T(1,128)}, u32[]{:S(2)}) copy-start(f32[1,4096]{1,0:T(1,128)} %param.16) | copy-start | bytes 49156
  690.1 7.5 collective-permute-start.4
  698.3 53.0 %all-gather.27.cloned.1.call-start = ((), (), s32[]{:S(2)}) async-start(), calls=%async_computation.12 | async-start | bytes 1310720 | tf_op jit(solution)/shard_map/all_gather | solution.py:117
  698.6 7.4 collective-permute-start.5
  706.0 0.7 copy-start.11
  706.7 84.3 %reduce-scatter.12.cloned.1.call-start = ((), (), s32[]{:S(2)}) async-start(), calls=%async_computation.14 | async-start | bytes 1310720 | tf_op jit(solution)/shard_map/reduce_scatter | solution.py:133
  727.1 27.7 %copy-start.18 = (bf16[1,128,4096]{2,1,0:T(8,128)(2,1)S(1)}, bf16[1,128,4096]{2,1,0:T(8,128)(2,1)}, u32[]{:S(2)}) copy-start(bf16[1,128,4096]{2,1,0:T(8,128)(2,1)} %all-gather.29.cloned.1.call-done) | copy-start | bytes 3145732
  762.4 28.6 %copy-start = (bf16[1,128,1024]{2,1,0:T(8,128)(2,1)S(1)}, bf16[1,128,1024]{2,1,0:T(8,128)(2,1)}, u32[]{:S(2)}) copy-start(bf16[1,128,1024]{2,1,0:T(8,128)(2,1)} %fusion.168) | copy-start | bytes 786436
  766.4 40.4 %copy-start.12 = (bf16[1,128,1024]{2,1,0:T(8,128)(2,1)S(1)}, bf16[1,128,1024]{2,1,0:T(8,128)(2,1)}, u32[]{:S(2)}) copy-start(bf16[1,128,1024]{2,1,0:T(8,128)(2,1)} %copy-done.11) | copy-start | bytes 786436
  766.4 67.6 %all-gather.33.cloned.1.call-start = ((), (), s32[]{:S(2)}) async-start(), calls=%async_computation.16 | async-start | bytes 1310720 | tf_op jit(solution)/shard_map/all_gather | solution.py:116
  791.0 15.7 %copy-start.7 = (bf16[1,128,1024]{2,1,0:T(8,128)(2,1)S(1)}, bf16[1,128,1024]{2,1,0:T(8,128)(2,1)}, u32[]{:S(2)}) copy-start(bf16[1,128,1024]{2,1,0:T(8,128)(2,1)} %reduce-scatter.12.cloned.1.call-done) | copy-start | bytes 786436
  798.5 61.3 %copy-start.30 = (f32[1,4096]{1,0:T(1,128)S(1)}, f32[1,4096]{1,0:T(1,128)}, u32[]{:S(2)}) copy-start(f32[1,4096]{1,0:T(1,128)} %param.16) | copy-start | bytes 49156
  798.5 7.4 collective-permute-start.6
  806.7 53.0 %all-gather.31.cloned.1.call-start = ((), (), s32[]{:S(2)}) async-start(), calls=%async_computation.15 | async-start | bytes 1310720 | tf_op jit(solution)/shard_map/all_gather | solution.py:117
  806.9 7.4 collective-permute-start.7
  814.3 0.7 copy-start.23
  815.1 83.5 %reduce-scatter.14.cloned.1.call-start = ((), (), s32[]{:S(2)}) async-start(), calls=%async_computation.17 | async-start | bytes 1310720 | tf_op jit(solution)/shard_map/reduce_scatter | solution.py:133
  835.5 27.7 %copy-start.19 = (bf16[1,128,4096]{2,1,0:T(8,128)(2,1)S(1)}, bf16[1,128,4096]{2,1,0:T(8,128)(2,1)}, u32[]{:S(2)}) copy-start(bf16[1,128,4096]{2,1,0:T(8,128)(2,1)} %all-gather.33.cloned.1.call-done) | copy-start | bytes 3145732
  873.9 24.6 %copy-start.4 = (bf16[1,128,1024]{2,1,0:T(8,128)(2,1)S(1)}, bf16[1,128,1024]{2,1,0:T(8,128)(2,1)}, u32[]{:S(2)}) copy-start(bf16[1,128,1024]{2,1,0:T(8,128)(2,1)} %fusion.167) | copy-start | bytes 786436
Sparse Core Ops, SparseCore 0:
  9.1 27.4 all-gather.34
  39.2 96.7 all-gather.36
  138.6 96.3 all-gather.38
  237.4 96.3 all-gather.40
  336.1 101.6 all-gather.42
  441.9 23.5 reduce-scatter.5
  481.4 27.0 all-gather.20
  510.3 24.0 all-gather.18
  549.6 24.4 reduce-scatter.7
  589.9 27.1 all-gather.24
  618.9 24.0 all-gather.22
  658.1 24.4 reduce-scatter.9
  698.4 27.0 all-gather.28
  727.2 24.0 all-gather.26
  766.5 24.4 reduce-scatter.11
  806.8 27.0 all-gather.32
  835.6 24.0 all-gather.30
  874.1 24.4 reduce-scatter.13
where the time goes:
time: 915 us; the launch traced here: 913 us
  waiting for transfers between devices  628 us (69%)
  local copies, waits for them, and re-layouts  109 us (12%)
  matrix products  71.5 us (8%)
  starting transfers between devices  30 us (3%)
  other arithmetic  27.8 us (3%)
  blocking collectives  25.6 us (3%)
  between operations  20.9 us (2%)
    reduce_scatter x5, waiting for transfers between devices, body(): lax.psum_scatter(partial_value.astype(jnp.bfloat16), 'tensor', scatter_di...  121 us
    gather x1, local copies, waits for them, and re-layouts, positional_bias(): bucket = jnp.take(bucket_row, key_pos - query_pos + (length - 1))  101 us
    all_gather x1, waiting for transfers between devices, body(): lax.all_gather(w_out[0], 'dp', axis=1, tiled=True)  100 us
    all_gather x4, waiting for transfers between devices, body(): lax.all_gather(memory_part, 'tensor', axis=2, tiled=True)  97.3 us
    all_gather x1, waiting for transfers between devices, body(): lax.all_gather(w_key[0], 'dp', axis=0, tiled=True)  95.7 us
    all_gather x1, waiting for transfers between devices, body(): lax.all_gather(w_query[0], 'dp', axis=0, tiled=True)  95.5 us
    all_gather x5, waiting for transfers between devices, body(): lax.all_gather(input_rows, 'tensor', axis=2, tiled=True)  66.7 us
    ppermute x8, waiting for transfers between devices, shifted(): lax.ppermute(value, axis, [(source, source + steps) for source in range(i...  30.5 us
  transfers between devices with their start and end apart: 26, of which 25 were waited for; matrix products, arithmetic and copies ran while one was open for 14% of the time, Pallas kernels for 0%

commit v1 on v0

--- a/solution.py
+++ b/solution.py
@@ -85,7 +85,9 @@
         lax.all_gather(w_query[0], "dp", axis=0, tiled=True),
         lax.all_gather(w_key[0], "dp", axis=0, tiled=True),
         lax.all_gather(w_value[0], "dp", axis=0, tiled=True),
-        lax.all_gather(w_out[0], "dp", axis=1, tiled=True),
+        jnp.concatenate(
+            lax.all_to_all(jnp.stack([w_out[0]] * lax.axis_size("dp")), "dp", 0, 0), axis=1
+        ),
     )
     score_bias = positional_bias(offset_bucket, bias_tables, section_id, length)
     query_pos = lax.broadcasted_iota(jnp.int32, (length, length), 0)

time: 915 us -> 852 us (0.931)
  waiting for transfers between devices: 628 us -> 550 us
  starting transfers between devices: 30 us -> 41.9 us
    all_gather x1 -> x0, waiting for transfers between devices: 100 us -> none  [body(): lax.all_gather(w_out[0], 'dp', axis=1, tiled=True)]
    all_gather x1, waiting for transfers between devices: 18.8 us -> 95.7 us  [body(): lax.all_gather(w_value[0], 'dp', axis=0, tiled=True)]
    all_gather x1, waiting for transfers between devices: 95.7 us -> 39.8 us  [body(): lax.all_gather(w_key[0], 'dp', axis=0, tiled=True)]
    all_to_all x0 -> x1, starting transfers between devices: none -> 11.9 us  [body(): lax.all_to_all(jnp.stack([w_out[0]] * lax.axis_size('dp')), 'dp', 0, 0)]
  transfers between devices with their start and end apart: 26 -> 26, of which waited for: 25 -> 24; matrix products, arithmetic and copies ran while one was open for 14% -> 15% of each run, Pallas kernels for 0% -> 0%
where the time goes in v1:
time: 852 us; the launch traced here: 851 us
  waiting for transfers between devices  550 us (65%)
  local copies, waits for them, and re-layouts  113 us (13%)
  matrix products  74 us (9%)
  starting transfers between devices  41.9 us (5%)
  other arithmetic  26.1 us (3%)
  blocking collectives  25.6 us (3%)
  between operations  20.3 us (2%)
    reduce_scatter x5, waiting for transfers between devices, body(): lax.psum_scatter(partial_value.astype(jnp.bfloat16), 'tensor', scatter_di...  121 us
    gather x1, local copies, waits for them, and re-layouts, positional_bias(): bucket = jnp.take(bucket_row, key_pos - query_pos + (length - 1))  101 us
    all_gather x4, waiting for transfers between devices, body(): lax.all_gather(memory_part, 'tensor', axis=2, tiled=True)  97.3 us
    all_gather x1, waiting for transfers between devices, body(): lax.all_gather(w_value[0], 'dp', axis=0, tiled=True)  95.7 us
    all_gather x1, waiting for transfers between devices, body(): lax.all_gather(w_query[0], 'dp', axis=0, tiled=True)  95.2 us
    all_gather x5, waiting for transfers between devices, body(): lax.all_gather(input_rows, 'tensor', axis=2, tiled=True)  68.8 us
    all_gather x1, waiting for transfers between devices, body(): lax.all_gather(w_key[0], 'dp', axis=0, tiled=True)  39.8 us
    ppermute x8, waiting for transfers between devices, shifted(): lax.ppermute(value, axis, [(source, source + steps) for source in range(i...  30.4 us
  transfers between devices with their start and end apart: 26, of which 24 were waited for; matrix products, arithmetic and copies ran while one was open for 15% of the time, Pallas kernels for 0%

profile of v1, /device:TPU:1, one launch (start us, length us, event | category | flops | bytes accessed | tf_op | source)
XLA Modules:
  0.0 850.8 jit_solution(1864489799745352289)
XLA Ops:
  6.5 1.8 select_select_fusion
  11.5 2.3 stack.3
  13.8 11.9 %all-to-all-start = ((bf16[16,512,256]{1,2,0:T(8,128)(2,1)}), bf16[16,512,256]{1,2,0:T(8,128)(2,1)}, u32[]{:S(2)}, u32[]{:S(2)}) async-start(bf16[16,512,256]{1,2,0:T(8,128)(2,1)} %stack.3), calls=%async_computation | async-start | bytes 8388608 | tf_op jit(solution)/shard_map/all_to_all | solution.py:89
  25.9 101.4 %gather_fusion = s32[16384]{0:T(1024)S(1)} fusion(s32[255]{0:T(256)S(1)} %bitcast.317, s32[16384]{0:T(1024)S(1)} %fusion.167), kind=kCustom, calls=%fused_computation | custom fusion | bytes 196608 | tf_op jit(solution)/shard_map/jit(_take)/gather | solution.py:22
  130.2 1.5 fusion.52
  131.8 39.8 %all-gather.39.cloned.1.call-done = bf16[1,4096,512]{2,1,0:T(8,128)(2,1)} async-done(((bf16[1,256,512]{2,1,0:T(8,128)(2,1)}), bf16[1,4096,512]{2,1,0:T(8,128)(2,1)}) %all-gather.39.cloned.1.call-update) | async-done | bytes 4194320 | tf_op jit(solution)/shard_map/all_gather | solution.py:86
  171.5 3.4 fusion.101
  175.0 95.2 %all-gather.37.cloned.1.call-done = bf16[1,4096,512]{2,1,0:T(8,128)(2,1)} async-done(((bf16[1,256,512]{2,1,0:T(8,128)(2,1)}), bf16[1,4096,512]{2,1,0:T(8,128)(2,1)}) %all-gather.37.cloned.1.call-update) | async-done | bytes 4194320 | tf_op jit(solution)/shard_map/all_gather | solution.py:85
  270.3 2.9 fusion.86
  273.3 95.7 %all-gather.35.cloned.1.call-done = bf16[1,4096,512]{2,1,0:T(8,128)(2,1)} async-done(((bf16[1,256,512]{2,1,0:T(8,128)(2,1)}), bf16[1,4096,512]{2,1,0:T(8,128)(2,1)}) %all-gather.35.cloned.1.call-update) | async-done | bytes 4194320 | tf_op jit(solution)/shard_map/all_gather | solution.py:87
  369.1 2.9 fusion.71
  372.9 4.7 fusion.5
  377.7 23.6 %reduce-scatter.6.cloned.1.call-done = bf16[1,128,1024]{2,1,0:T(8,128)(2,1)} async-done(((bf16[1,128,4096]{2,1,0:T(8,128)(2,1)}), bf16[1,128,1024]{2,1,0:T(8,128)(2,1)}) %reduce-scatter.6.cloned.1.call-update) | async-done | bytes 262160 | tf_op jit(solution)/shard_map/reduce_scatter | solution.py:135
  402.5 5.1 psum.35
  408.8 3.1 collective-permute-start
  411.9 4.3 collective-permute-done
  417.2 4.1 collective-permute-start.1
  421.4 3.3 collective-permute-done.1
  427.4 16.9 %all-gather.19.cloned.1.call-done = bf16[1,128,4096]{2,1,0:T(8,128)(2,1)} async-done(((bf16[1,128,1024]{2,1,0:T(8,128)(2,1)}), bf16[1,128,4096]{2,1,0:T(8,128)(2,1)}) %all-gather.19.cloned.1.call-update) | async-done | bytes 1048592 | tf_op jit(solution)/shard_map/all_gather | solution.py:118
  444.3 1.5 fusion.40
  445.9 24.4 %all-gather.17.cloned.1.call-done = bf16[1,128,4096]{2,1,0:T(8,128)(2,1)} async-done(((bf16[1,128,1024]{2,1,0:T(8,128)(2,1)}), bf16[1,128,4096]{2,1,0:T(8,128)(2,1)}) %all-gather.17.cloned.1.call-update) | async-done | bytes 1048592 | tf_op jit(solution)/shard_map/all_gather | solution.py:119
  470.3 3.3 fusion.104
  473.7 2.9 fusion.89
  477.2 3.3 fusion.74
  480.9 4.7 fusion.6
  485.7 24.5 %reduce-scatter.8.cloned.1.call-done = bf16[1,128,1024]{2,1,0:T(8,128)(2,1)} async-done(((bf16[1,128,4096]{2,1,0:T(8,128)(2,1)}), bf16[1,128,1024]{2,1,0:T(8,128)(2,1)}) %reduce-scatter.8.cloned.1.call-update) | async-done | bytes 262160 | tf_op jit(solution)/shard_map/reduce_scatter | solution.py:135
  511.4 5.1 psum.36
  517.7 3.3 collective-permute-start.2
  521.0 4.1 collective-permute-done.2
  526.1 4.1 collective-permute-start.3
  530.2 3.3 collective-permute-done.3
  535.5 17.7 %all-gather.23.cloned.1.call-done = bf16[1,128,4096]{2,1,0:T(8,128)(2,1)} async-done(((bf16[1,128,1024]{2,1,0:T(8,128)(2,1)}), bf16[1,128,4096]{2,1,0:T(8,128)(2,1)}) %all-gather.23.cloned.1.call-update) | async-done | bytes 1048592 | tf_op jit(solution)/shard_map/all_gather | solution.py:118
  554.7 24.3 %all-gather.21.cloned.1.call-done = bf16[1,128,4096]{2,1,0:T(8,128)(2,1)} async-done(((bf16[1,128,1024]{2,1,0:T(8,128)(2,1)}), bf16[1,128,4096]{2,1,0:T(8,128)(2,1)}) %all-gather.21.cloned.1.call-update) | async-done | bytes 1048592 | tf_op jit(solution)/shard_map/all_gather | solution.py:119
  579.0 3.3 fusion.107
  582.4 3.0 fusion.92
  585.9 3.3 fusion.77
  589.6 4.7 fusion.7
  594.4 24.5 %reduce-scatter.10.cloned.1.call-done = bf16[1,128,1024]{2,1,0:T(8,128)(2,1)} async-done(((bf16[1,128,4096]{2,1,0:T(8,128)(2,1)}), bf16[1,128,1024]{2,1,0:T(8,128)(2,1)}) %reduce-scatter.10.cloned.1.call-update) | async-done | bytes 262160 | tf_op jit(solution)/shard_map/reduce_scatter | solution.py:135
  620.1 5.2 psum.37
  626.4 3.1 collective-permute-start.4
  629.5 4.3 collective-permute-done.4
  634.8 4.1 collective-permute-start.5
  639.0 3.3 collective-permute-done.5
  644.9 17.0 %all-gather.27.cloned.1.call-done = bf16[1,128,4096]{2,1,0:T(8,128)(2,1)} async-done(((bf16[1,128,1024]{2,1,0:T(8,128)(2,1)}), bf16[1,128,4096]{2,1,0:T(8,128)(2,1)}) %all-gather.27.cloned.1.call-update) | async-done | bytes 1048592 | tf_op jit(solution)/shard_map/all_gather | solution.py:118
  663.5 24.4 %all-gather.25.cloned.1.call-done = bf16[1,128,4096]{2,1,0:T(8,128)(2,1)} async-done(((bf16[1,128,1024]{2,1,0:T(8,128)(2,1)}), bf16[1,128,4096]{2,1,0:T(8,128)(2,1)}) %all-gather.25.cloned.1.call-update) | async-done | bytes 1048592 | tf_op jit(solution)/shard_map/all_gather | solution.py:119
  687.9 3.3 fusion.110
  691.3 2.9 fusion.95
  694.8 3.3 fusion.80
  698.5 4.7 fusion.8
  703.3 24.5 %reduce-scatter.12.cloned.1.call-done = bf16[1,128,1024]{2,1,0:T(8,128)(2,1)} async-done(((bf16[1,128,4096]{2,1,0:T(8,128)(2,1)}), bf16[1,128,1024]{2,1,0:T(8,128)(2,1)}) %reduce-scatter.12.cloned.1.call-update) | async-done | bytes 262160 | tf_op jit(solution)/shard_map/reduce_scatter | solution.py:135
  729.0 5.1 psum.38
  735.3 3.1 collective-permute-start.6
  738.4 4.4 collective-permute-done.6
  743.8 4.1 collective-permute-start.7
  747.9 3.5 collective-permute-done.7
  753.7 17.1 %all-gather.31.cloned.1.call-done = bf16[1,128,4096]{2,1,0:T(8,128)(2,1)} async-done(((bf16[1,128,1024]{2,1,0:T(8,128)(2,1)}), bf16[1,128,4096]{2,1,0:T(8,128)(2,1)}) %all-gather.31.cloned.1.call-update) | async-done | bytes 1048592 | tf_op jit(solution)/shard_map/all_gather | solution.py:118
  772.3 24.3 %all-gather.29.cloned.1.call-done = bf16[1,128,4096]{2,1,0:T(8,128)(2,1)} async-done(((bf16[1,128,1024]{2,1,0:T(8,128)(2,1)}), bf16[1,128,4096]{2,1,0:T(8,128)(2,1)}) %all-gather.29.cloned.1.call-update) | async-done | bytes 1048592 | tf_op jit(solution)/shard_map/all_gather | solution.py:119
  796.6 3.3 fusion.113
  800.0 3.0 fusion.98
  803.5 3.0 fusion.83
  806.9 4.7 fusion.9
  812.4 23.8 %reduce-scatter.14.cloned.1.call-done = bf16[1,128,1024]{2,1,0:T(8,128)(2,1)} async-done(((bf16[1,128,4096]{2,1,0:T(8,128)(2,1)}), bf16[1,128,1024]{2,1,0:T(8,128)(2,1)}) %reduce-scatter.14.cloned.1.call-update) | async-done | bytes 262160 | tf_op jit(solution)/shard_map/reduce_scatter | solution.py:135
  837.3 5.1 psum.39
  842.4 1.8 fusion.161
  (172 shorter events, 34.8 us)
Async XLA Ops:
  6.5 123.7 %all-gather.33.cloned.1.call-start = ((), (), s32[]{:S(2)}) async-start(), calls=%async_computation.19 | async-start | bytes 1310720 | tf_op jit(solution)/shard_map/all_gather | solution.py:118
  8.3 163.2 %all-gather.39.cloned.1.call-start = ((), (), s32[]{:S(2)}) async-start(), calls=%async_computation.22 | async-start | bytes 4456448 | tf_op jit(solution)/shard_map/all_gather | solution.py:86
  9.1 261.2 %all-gather.37.cloned.1.call-start = ((), (), s32[]{:S(2)}) async-start(), calls=%async_computation.21 | async-start | bytes 4456448 | tf_op jit(solution)/shard_map/all_gather | solution.py:85
  9.8 359.3 %all-gather.35.cloned.1.call-start = ((), (), s32[]{:S(2)}) async-start(), calls=%async_computation.20 | async-start | bytes 4456448 | tf_op jit(solution)/shard_map/all_gather | solution.py:87
  13.8 12.0 %copy-start.26 = (s32[2,255]{1,0:T(2,128)S(1)}, s32[2,255]{1,0:T(2,128)}, u32[]{:S(2)}) copy-start(s32[2,255]{1,0:T(2,128)} %param.14) | copy-start | bytes 6124
  13.8 359.0 %all-to-all-start = ((bf16[16,512,256]{1,2,0:T(8,128)(2,1)}), bf16[16,512,256]{1,2,0:T(8,128)(2,1)}, u32[]{:S(2)}, u32[]{:S(2)}) async-start(bf16[16,512,256]{1,2,0:T(8,128)(2,1)} %stack.3), calls=%async_computation | async-start | bytes 8388608 | tf_op jit(solution)/shard_map/all_to_all | solution.py:89
  25.7 375.6 %reduce-scatter.6.cloned.1.call-start = ((), (), s32[]{:S(2)}) async-start(), calls=%async_computation.6 | async-start | bytes 1310720 | tf_op jit(solution)/shard_map/reduce_scatter | solution.py:135
  25.9 101.5 %copy-start.25 = (f32[2,32,8]{1,2,0:T(8,128)S(1)}, f32[2,32,8]{1,2,0:T(8,128)}, u32[]{:S(2)}) copy-start(f32[2,32,8]{1,2,0:T(8,128)} %param.15) | copy-start | bytes 6148
  25.9 102.4 %copy-start.24 = (s32[2,2,1]{1,2,0:T(1,128)S(1)}, s32[2,2,1]{1,2,0:T(1,128)}, u32[]{:S(2)}) copy-start(s32[2,2,1]{1,2,0:T(1,128)} %param.13) | copy-start | bytes 52
  127.3 44.2 %copy-start.27 = (f32[1,4096]{1,0:T(1,128)S(1)}, f32[1,4096]{1,0:T(1,128)}, u32[]{:S(2)}) copy-start(f32[1,4096]{1,0:T(1,128)} %param.16) | copy-start | bytes 49156
  171.5 98.7 %copy-start.17 = (bf16[1,1,128,4096]{3,2,1,0:T(8,128)(2,1)S(1)}, bf16[1,1,128,4096]{3,2,1,0:T(8,128)(2,1)}, u32[]{:S(2)}) copy-start(bf16[1,1,128,4096]{3,2,1,0:T(8,128)(2,1)} %all-gather.33.cloned.1.call-done) | copy-start | bytes 3145732
  372.9 28.5 %copy-start.3 = (bf16[1,1,128,1024]{3,2,1,0:T(8,128)(2,1)S(1)}, bf16[1,1,128,1024]{3,2,1,0:T(8,128)(2,1)}, u32[]{:S(2)}) copy-start(bf16[1,1,128,1024]{3,2,1,0:T(8,128)(2,1)} %select_select_fusion) | copy-start | bytes 786436
  377.6 30.1 %copy-start.22 = (f32[1024]{0:T(1024)S(1)}, f32[1024]{0:T(1024)}, u32[]{:S(2)}) copy-start(f32[1024]{0:T(1024)} %param.17) | copy-start | bytes 12292
  377.6 38.6 %copy-start.5 = (bf16[2,1,128,1024]{3,2,1,0:T(8,128)(2,1)S(1)}, bf16[2,1,128,1024]{3,2,1,0:T(8,128)(2,1)}, u32[]{:S(2)}) copy-start(bf16[2,1,128,1024]{3,2,1,0:T(8,128)(2,1)} %param.12) | copy-start | bytes 1572868
  377.6 38.6 %copy-start.6 = (bf16[2,1,128,1024]{3,2,1,0:T(8,128)(2,1)S(1)}, bf16[2,1,128,1024]{3,2,1,0:T(8,128)(2,1)}, u32[]{:S(2)}) copy-start(bf16[2,1,128,1024]{3,2,1,0:T(8,128)(2,1)} %param.11) | copy-start | bytes 1572868
  377.6 66.7 %all-gather.19.cloned.1.call-start = ((), (), s32[]{:S(2)}) async-start(), calls=%async_computation.8 | async-start | bytes 1310720 | tf_op jit(solution)/shard_map/all_gather | solution.py:118
  401.3 15.8 %copy-start.10 = (bf16[1,128,1024]{2,1,0:T(8,128)(2,1)S(1)}, bf16[1,128,1024]{2,1,0:T(8,128)(2,1)}, u32[]{:S(2)}) copy-start(bf16[1,128,1024]{2,1,0:T(8,128)(2,1)} %reduce-scatter.6.cloned.1.call-done) | copy-start | bytes 786436
  408.8 7.4 collective-permute-start
  417.0 53.2 %all-gather.17.cloned.1.call-start = ((), (), s32[]{:S(2)}) async-start(), calls=%async_computation.7 | async-start | bytes 1310720 | tf_op jit(solution)/shard_map/all_gather | solution.py:119
  417.2 7.4 collective-permute-start.1
  424.6 0.7 copy-start.13
  425.4 84.9 %reduce-scatter.8.cloned.1.call-start = ((), (), s32[]{:S(2)}) async-start(), calls=%async_computation.9 | async-start | bytes 1310720 | tf_op jit(solution)/shard_map/reduce_scatter | solution.py:135
  445.8 27.8 %copy-start.20 = (bf16[1,128,4096]{2,1,0:T(8,128)(2,1)S(1)}, bf16[1,128,4096]{2,1,0:T(8,128)(2,1)}, u32[]{:S(2)}) copy-start(bf16[1,128,4096]{2,1,0:T(8,128)(2,1)} %all-gather.19.cloned.1.call-done) | copy-start | bytes 3145732
  480.9 29.4 %copy-start.1 = (bf16[1,128,1024]{2,1,0:T(8,128)(2,1)S(1)}, bf16[1,128,1024]{2,1,0:T(8,128)(2,1)}, u32[]{:S(2)}) copy-start(bf16[1,128,1024]{2,1,0:T(8,128)(2,1)} %fusion.165) | copy-start | bytes 786436
  485.6 40.3 %copy-start.14 = (bf16[1,128,1024]{2,1,0:T(8,128)(2,1)S(1)}, bf16[1,128,1024]{2,1,0:T(8,128)(2,1)}, u32[]{:S(2)}) copy-start(bf16[1,128,1024]{2,1,0:T(8,128)(2,1)} %copy-done.13) | copy-start | bytes 786436
  485.6 67.6 %all-gather.23.cloned.1.call-start = ((), (), s32[]{:S(2)}) async-start(), calls=%async_computation.11 | async-start | bytes 1310720 | tf_op jit(solution)/shard_map/all_gather | solution.py:118
  510.2 15.7 %copy-start.8 = (bf16[1,128,1024]{2,1,0:T(8,128)(2,1)S(1)}, bf16[1,128,1024]{2,1,0:T(8,128)(2,1)}, u32[]{:S(2)}) copy-start(bf16[1,128,1024]{2,1,0:T(8,128)(2,1)} %reduce-scatter.8.cloned.1.call-done) | copy-start | bytes 786436
  517.7 7.4 collective-permute-start.2
  525.9 53.1 %all-gather.21.cloned.1.call-start = ((), (), s32[]{:S(2)}) async-start(), calls=%async_computation.10 | async-start | bytes 1310720 | tf_op jit(solution)/shard_map/all_gather | solution.py:119
  526.1 7.4 collective-permute-start.3
  533.5 0.7 copy-start.15
  534.2 84.7 %reduce-scatter.10.cloned.1.call-start = ((), (), s32[]{:S(2)}) async-start(), calls=%async_computation.12 | async-start | bytes 1310720 | tf_op jit(solution)/shard_map/reduce_scatter | solution.py:135
  554.7 27.7 %copy-start.21 = (bf16[1,128,4096]{2,1,0:T(8,128)(2,1)S(1)}, bf16[1,128,4096]{2,1,0:T(8,128)(2,1)}, u32[]{:S(2)}) copy-start(bf16[1,128,4096]{2,1,0:T(8,128)(2,1)} %all-gather.23.cloned.1.call-done) | copy-start | bytes 3145732
  589.6 29.3 %copy-start.2 = (bf16[1,128,1024]{2,1,0:T(8,128)(2,1)S(1)}, bf16[1,128,1024]{2,1,0:T(8,128)(2,1)}, u32[]{:S(2)}) copy-start(bf16[1,128,1024]{2,1,0:T(8,128)(2,1)} %fusion.164) | copy-start | bytes 786436
  594.3 40.3 %copy-start.16 = (bf16[1,128,1024]{2,1,0:T(8,128)(2,1)S(1)}, bf16[1,128,1024]{2,1,0:T(8,128)(2,1)}, u32[]{:S(2)}) copy-start(bf16[1,128,1024]{2,1,0:T(8,128)(2,1)} %copy-done.15) | copy-start | bytes 786436
  594.4 67.6 %all-gather.27.cloned.1.call-start = ((), (), s32[]{:S(2)}) async-start(), calls=%async_computation.14 | async-start | bytes 1310720 | tf_op jit(solution)/shard_map/all_gather | solution.py:118
  618.9 15.8 %copy-start.9 = (bf16[1,128,1024]{2,1,0:T(8,128)(2,1)S(1)}, bf16[1,128,1024]{2,1,0:T(8,128)(2,1)}, u32[]{:S(2)}) copy-start(bf16[1,128,1024]{2,1,0:T(8,128)(2,1)} %reduce-scatter.10.cloned.1.call-done) | copy-start | bytes 786436
  626.4 7.4 collective-permute-start.4
  634.6 53.3 %all-gather.25.cloned.1.call-start = ((), (), s32[]{:S(2)}) async-start(), calls=%async_computation.13 | async-start | bytes 1310720 | tf_op jit(solution)/shard_map/all_gather | solution.py:119
  634.8 7.4 collective-permute-start.5
  642.2 0.7 copy-start.11
  643.0 84.9 %reduce-scatter.12.cloned.1.call-start = ((), (), s32[]{:S(2)}) async-start(), calls=%async_computation.15 | async-start | bytes 1310720 | tf_op jit(solution)/shard_map/reduce_scatter | solution.py:135
  663.5 27.8 %copy-start.19 = (bf16[1,128,4096]{2,1,0:T(8,128)(2,1)S(1)}, bf16[1,128,4096]{2,1,0:T(8,128)(2,1)}, u32[]{:S(2)}) copy-start(bf16[1,128,4096]{2,1,0:T(8,128)(2,1)} %all-gather.27.cloned.1.call-done) | copy-start | bytes 3145732
  698.5 29.4 %copy-start = (bf16[1,128,1024]{2,1,0:T(8,128)(2,1)S(1)}, bf16[1,128,1024]{2,1,0:T(8,128)(2,1)}, u32[]{:S(2)}) copy-start(bf16[1,128,1024]{2,1,0:T(8,128)(2,1)} %fusion.163) | copy-start | bytes 786436
  703.2 40.4 %copy-start.12 = (bf16[1,128,1024]{2,1,0:T(8,128)(2,1)S(1)}, bf16[1,128,1024]{2,1,0:T(8,128)(2,1)}, u32[]{:S(2)}) copy-start(bf16[1,128,1024]{2,1,0:T(8,128)(2,1)} %copy-done.11) | copy-start | bytes 786436
  703.2 67.6 %all-gather.31.cloned.1.call-start = ((), (), s32[]{:S(2)}) async-start(), calls=%async_computation.17 | async-start | bytes 1310720 | tf_op jit(solution)/shard_map/all_gather | solution.py:118
  727.8 15.8 %copy-start.7 = (bf16[1,128,1024]{2,1,0:T(8,128)(2,1)S(1)}, bf16[1,128,1024]{2,1,0:T(8,128)(2,1)}, u32[]{:S(2)}) copy-start(bf16[1,128,1024]{2,1,0:T(8,128)(2,1)} %reduce-scatter.12.cloned.1.call-done) | copy-start | bytes 786436
  735.3 7.5 collective-permute-start.6
  743.6 53.0 %all-gather.29.cloned.1.call-start = ((), (), s32[]{:S(2)}) async-start(), calls=%async_computation.16 | async-start | bytes 1310720 | tf_op jit(solution)/shard_map/all_gather | solution.py:119
  743.8 7.6 collective-permute-start.7
  751.4 0.7 copy-start.23
  752.2 84.0 %reduce-scatter.14.cloned.1.call-start = ((), (), s32[]{:S(2)}) async-start(), calls=%async_computation.18 | async-start | bytes 1310720 | tf_op jit(solution)/shard_map/reduce_scatter | solution.py:135
  772.3 27.7 %copy-start.18 = (bf16[1,128,4096]{2,1,0:T(8,128)(2,1)S(1)}, bf16[1,128,4096]{2,1,0:T(8,128)(2,1)}, u32[]{:S(2)}) copy-start(bf16[1,128,4096]{2,1,0:T(8,128)(2,1)} %all-gather.31.cloned.1.call-done) | copy-start | bytes 3145732
  811.5 24.6 %copy-start.4 = (bf16[1,128,1024]{2,1,0:T(8,128)(2,1)S(1)}, bf16[1,128,1024]{2,1,0:T(8,128)(2,1)}, u32[]{:S(2)}) copy-start(bf16[1,128,1024]{2,1,0:T(8,128)(2,1)} %fusion.162) | copy-start | bytes 786436
Sparse Core Ops, SparseCore 0:
  9.1 44.6 all-gather.32
  56.4 115.0 all-gather.38
  174.1 96.0 all-gather.36
  272.7 96.3 all-gather.34
  377.8 23.5 reduce-scatter.5
  417.2 27.1 all-gather.18
  446.1 24.0 all-gather.16
  485.7 24.4 reduce-scatter.7
  526.0 27.1 all-gather.22
  554.9 24.0 all-gather.20
  594.5 24.3 reduce-scatter.9
  634.7 27.1 all-gather.26
  663.7 24.0 all-gather.24
  703.3 24.4 reduce-scatter.11
  743.7 27.0 all-gather.30
  772.5 24.0 all-gather.28
  811.7 24.4 reduce-scatter.13
